TPU v7x, 32 devices: a whole 2x2x4 slice. The times are simulated.
32 devices in a mesh: bucket: 16 (over z, y, x), seq: 2 (over core).
Axes of the slice: x: 2, y: 2, z: 4, core: 2. Of those that a mesh axis runs over, the one named last changes fastest.
Arguments:
- tokens: bfloat16 [64, 512, 384], P('bucket', 'seq'), may hold values from -6 to 6
- cotangent: bfloat16 [64, 512, 384], P('bucket', 'seq'), may hold values from -6 to 6
- segment_ids: int32 [64, 512], P('bucket'), may hold values from 0 to 7, never falling along the last dimension, each value on 1 to 256 neighbouring positions
- pad_counts: int32 [64], P('bucket'), may hold values from 0 to 128
- timesteps: int32 [64, 8], P('bucket'), may hold values from 0 to 999
- classes: int32 [64, 8], P('bucket'), may hold values from 0 to 999
- head_mask: int32 [64, 8, 6], P('bucket'), may hold values 0 or 1
- channel_mask: int32 [64, 8, 24], P('bucket'), may hold values 0 or 1
- keep_mask: int32 [64, 512], P('bucket', 'seq'), may hold values 0 or 1
- class_table: bfloat16 [1000, 384], replicated, may hold values from -6 to 6
- w_ada: bfloat16 [384, 2304], P('bucket', 'seq'), may hold values from -0.3125 to 0.3125
- b_ada: bfloat16 [2304], P('seq'), may hold values from -2 to 2
- w_qkv: bfloat16 [384, 1152], replicated, may hold values from -0.3125 to 0.3125
- bias_qv: bfloat16 [768], replicated, may hold values from -2 to 2
- w_proj: bfloat16 [384, 384], replicated, may hold values from -2.5 to 2.5
- b_proj: bfloat16 [384], replicated, may hold values from -2 to 2
- w_fc1: bfloat16 [384, 1536], replicated, may hold values from -0.3125 to 0.3125
- b_fc1: bfloat16 [1536], replicated, may hold values from -2 to 2
- w_fc2: bfloat16 [1536, 384], replicated, may hold values from -0.15625 to 0.15625
- b_fc2: bfloat16 [384], replicated, may hold values from -2 to 2
- w_router: bfloat16 [384], replicated, may hold values from -0.3125 to 0.3125
Outputs:
- output: bfloat16 [64, 512, 384], P('bucket', 'seq')
- grad_tokens: bfloat16 [64, 512, 384], P('bucket', 'seq')
- grad_class_table: float32 [1000, 384], P(None, 'bucket')
- grad_w_ada: float32 [384, 2304], P('bucket', 'seq')
- grad_b_ada: float32 [2, 1152], P('seq', 'bucket')
- grad_w_qkv: float32 [384, 1152], P(None, 'bucket')
- grad_bias_qv: float32 [768], P('bucket')
- grad_w_proj: float32 [384, 384], P(None, 'bucket')
- grad_b_proj: float32 [384], P('bucket')
- grad_w_fc1: float32 [384, 1536], P(None, 'bucket')
- grad_b_fc1: float32 [1536], P('bucket')
- grad_w_fc2: float32 [1536, 384], P('bucket')
- grad_b_fc2: float32 [384], P('bucket')
- grad_w_router: float32 [384], P('bucket')
Inputs may be any that keep to these rules, and one draw needn't show every extreme that they name: `segment_ids`: crop numbers never fall along a row; each crop has 1 to 256 tokens and one has exactly 256. The padding tokens are the last pad_counts[r] tokens of row r.
All inputs are finite; a program needn't handle non-finite values. No bound on the sum of `head_mask` or of `channel_mask` or of `keep_mask` on one device may be relied on, other than what follows from the above.
Results may differ from a plain program's by a relative error of at most 0.014.
The roundings to bfloat16 on the way count: a program that leaves them out, or rounds other values in their place, can miss the bound.
Values may be sent and summed in bfloat16 or wider, within the bound.
No kernel may reach another device: no remote copies, remote signals or barrier semaphores. Data moves between devices by JAX's collectives and lax.ppermute only.
A program may use at most 192 MiB of HBM per device.

v0:
```python
from functools import partial
import math
import jax
import jax.numpy as jnp
from jax import lax
from jax.sharding import PartitionSpec as P

D = 384
HEADS = 6
HEAD_DIM = 64
FF = 1536
NCLASS = 1000
CGROUPS = 24
CROPS = 8
HIGHEST_PRECISION = lax.Precision.HIGHEST
EPSILON = 1e-06
NEGATIVE = -1e30


def exact(form, left, right):
    return jnp.einsum(form, left, right, precision=HIGHEST_PRECISION)


def layer_norm(values_in):
    centred = values_in - jnp.mean(values_in, -1, keepdims=True)
    variance = jnp.mean(centred * centred, -1, keepdims=True)
    return centred * lax.rsqrt(variance + EPSILON)


def time_embed(timesteps):
    half_width = D // 2
    frequency = jnp.exp(-math.log(10000.0) * jnp.arange(half_width, dtype=jnp.float32) / half_width)
    angles = timesteps.astype(jnp.float32)[..., None] * frequency
    return jnp.concatenate([jnp.cos(angles), jnp.sin(angles)], -1)


def first_norm(token_in, shift_in, scale_in):
    return layer_norm(token_in) * (1.0 + scale_in) + shift_in


def heads_view(matrix):
    return matrix.reshape(matrix.shape[0], HEADS, HEAD_DIM)


def body(
    tokens,
    cotangent,
    segment_ids,
    pad_counts,
    timesteps,
    classes,
    head_mask,
    channel_mask,
    keep_mask,
    class_table,
    w_ada,
    b_ada,
    w_qkv,
    bias_qv,
    w_proj,
    b_proj,
    w_fc1,
    b_fc1,
    w_fc2,
    b_fc2,
    w_router,
):
    row_count, local_len, width_all = tokens.shape
    full_len = local_len * lax.axis_size("seq")
    first_pos = lax.axis_index("seq") * local_len
    token_count = row_count * local_len
    shape_three = (row_count, local_len, D)
    position = jnp.arange(full_len, dtype=jnp.int32)
    live_row = position[None, :] < (full_len - pad_counts)[:, None]
    attend_keys = jnp.where(live_row, segment_ids, -1)
    attend_query = lax.dynamic_slice_in_dim(attend_keys, first_pos, local_len, 1)
    live_here = lax.dynamic_slice_in_dim(live_row.astype(jnp.float32), first_pos, local_len, 1)
    crop_here = lax.dynamic_slice_in_dim(segment_ids, first_pos, local_len, 1)
    crop_hot = (crop_here[:, :, None] == jnp.arange(CROPS, dtype=jnp.int32)).astype(jnp.float32)
    class_hot = (classes[:, :, None] == jnp.arange(NCLASS, dtype=jnp.int32)).astype(jnp.float32)
    ada_full = lax.all_gather(w_ada, "bucket", axis=0, tiled=True)
    condition = time_embed(timesteps) + exact(
        "rcn,nd->rcd", class_hot, class_table.astype(jnp.float32)
    )
    silu_value, pull_silu = jax.vjp(jax.nn.silu, condition)
    silu_low = silu_value.astype(jnp.bfloat16)
    mod_part = jnp.einsum(
        "rcd,dm->rcm", silu_low, ada_full, preferred_element_type=jnp.float32
    ) + b_ada.astype(jnp.float32)
    modulation = lax.all_gather(mod_part, "seq", axis=2, tiled=True)
    per_token = exact("rlc,rcm->rlm", crop_hot, modulation)
    shift_one, scale_one, gate_one, shift_two, scale_two, gate_two = jnp.split(
        per_token, 6, axis=-1
    )
    token_float = tokens.astype(jnp.float32)
    hidden_one, pull_first = jax.vjp(first_norm, token_float, shift_one, scale_one)
    hidden_low = hidden_one.astype(jnp.bfloat16).reshape(token_count, D)
    projected = jnp.dot(hidden_low, w_qkv, preferred_element_type=jnp.float32)
    bias_float = bias_qv.astype(jnp.float32)
    query = (projected[:, :D] + bias_float[:D]).astype(jnp.bfloat16).reshape(shape_three)
    key_here = projected[:, D : 2 * D].astype(jnp.bfloat16).reshape(shape_three)
    value_here = (projected[:, 2 * D :] + bias_float[D:]).astype(jnp.bfloat16).reshape(shape_three)
    key_rows, value_rows = (
        lax.all_gather(key_here, "seq", axis=1, tiled=True),
        lax.all_gather(value_here, "seq", axis=1, tiled=True),
    )
    same_crop = attend_query[:, :, None] == attend_keys[:, None, :]
    score_scale = HEAD_DIM ** (-0.5)

    def raw_scores(query_row, key_row, same_row):
        scores = (
            jnp.einsum(
                "qhe,khe->hqk",
                heads_view(query_row),
                heads_view(key_row),
                preferred_element_type=jnp.float32,
            )
            * score_scale
        )
        return jnp.where(same_row[None], scores, NEGATIVE)

    def attend(item):
        query_row, key_row, value_row, same_row = item
        scores = raw_scores(query_row, key_row, same_row)
        row_max = jnp.max(scores, -1, keepdims=True)
        numerator = jnp.exp(scores - row_max)
        denominator = jnp.sum(numerator, -1, keepdims=True)
        probability = (numerator / denominator).astype(jnp.bfloat16)
        mixed_heads = jnp.einsum(
            "hqk,khe->qhe", probability, heads_view(value_row), preferred_element_type=jnp.float32
        )
        return (mixed_heads, (row_max + jnp.log(denominator))[..., 0])

    mixed_heads, log_total = lax.map(attend, (query, key_rows, value_rows, same_crop))
    head_scale = exact("rlc,rch->rlh", crop_hot, head_mask.astype(jnp.float32))[..., None]
    attended = (mixed_heads * head_scale).astype(jnp.bfloat16).reshape(token_count, D)
    branch = (
        jnp.dot(attended, w_proj, preferred_element_type=jnp.float32) + b_proj.astype(jnp.float32)
    ).reshape(shape_three)
    live_column = live_here[..., None]

    def second_norm(token_in, branch_in, gate_in, shift_in, scale_in):
        residual_in = token_in + live_column * gate_in * branch_in
        return (residual_in, layer_norm(residual_in) * (1.0 + scale_in) + shift_in)

    (residual, hidden_two), pull_second = jax.vjp(
        second_norm, token_float, branch, gate_one, shift_two, scale_two
    )
    second_low = hidden_two.astype(jnp.bfloat16).reshape(token_count, D)
    router_rate = jax.nn.sigmoid(jnp.dot(second_low, w_router, preferred_element_type=jnp.float32))
    pre_act = jnp.dot(second_low, w_fc1, preferred_element_type=jnp.float32) + b_fc1.astype(
        jnp.float32
    )
    chans_tok = exact(
        "rlc,rcf->rlf",
        crop_hot,
        jnp.repeat(channel_mask.astype(jnp.float32), FF // CGROUPS, axis=-1),
    ).reshape(token_count, FF)
    gelu_out, pull_gelu = jax.vjp(partial(jax.nn.gelu, approximate=True), pre_act)
    activation = (gelu_out * chans_tok).astype(jnp.bfloat16)
    mlp_out = jnp.dot(activation, w_fc2, preferred_element_type=jnp.float32) + b_fc2.astype(
        jnp.float32
    )
    keep_live = (live_here * keep_mask.astype(jnp.float32)).reshape(token_count)
    branch_coef = keep_live * router_rate
    gate_flat = gate_two.reshape(token_count, D)
    outcome = residual.reshape(token_count, D) + branch_coef[:, None] * gate_flat * mlp_out
    output = outcome.astype(jnp.bfloat16).reshape(shape_three)
    grad_out = cotangent.astype(jnp.float32).reshape(token_count, D)
    grad_mlp = (grad_out * branch_coef[:, None] * gate_flat).astype(jnp.bfloat16)
    grad_gate_two = grad_out * branch_coef[:, None] * mlp_out
    grad_rate = jnp.sum(grad_out * gate_flat * mlp_out, -1) * keep_live
    grad_logit = grad_rate * router_rate * (1.0 - router_rate)
    grad_w_fc2 = jnp.einsum("nf,nd->fd", activation, grad_mlp, preferred_element_type=jnp.float32)
    grad_b_fc2 = jnp.sum(grad_mlp.astype(jnp.float32), 0)
    grad_act = jnp.einsum("nd,fd->nf", grad_mlp, w_fc2, preferred_element_type=jnp.float32)
    grad_pre = pull_gelu(grad_act * chans_tok)[0].astype(jnp.bfloat16)
    grad_w_fc1 = jnp.einsum("nd,nf->df", second_low, grad_pre, preferred_element_type=jnp.float32)
    grad_b_fc1 = jnp.sum(grad_pre.astype(jnp.float32), 0)
    grad_w_router = exact("nd,n->d", second_low.astype(jnp.float32), grad_logit)
    grad_hidden_two = (
        jnp.einsum("nf,df->nd", grad_pre, w_fc1, preferred_element_type=jnp.float32)
        + grad_logit[:, None] * w_router.astype(jnp.float32)[None, :]
    )
    part_fc1, part_bfc1, part_fc2, part_bfc2, part_router = (
        lax.psum_scatter(grad_w_fc1, "bucket", scatter_dimension=1, tiled=True),
        lax.psum_scatter(grad_b_fc1, "bucket", scatter_dimension=0, tiled=True),
        lax.psum_scatter(grad_w_fc2, "bucket", scatter_dimension=0, tiled=True),
        lax.psum_scatter(grad_b_fc2, "bucket", scatter_dimension=0, tiled=True),
        lax.psum_scatter(grad_w_router, "bucket", scatter_dimension=0, tiled=True),
    )
    mlp_sums = (
        lax.psum(part_fc1.astype(jnp.bfloat16), "seq").astype(jnp.float32),
        lax.psum(part_bfc1.astype(jnp.bfloat16), "seq").astype(jnp.float32),
        lax.psum(part_fc2.astype(jnp.bfloat16), "seq").astype(jnp.float32),
        lax.psum(part_bfc2.astype(jnp.bfloat16), "seq").astype(jnp.float32),
        lax.psum(part_router.astype(jnp.bfloat16), "seq").astype(jnp.float32),
    )
    grad_token_one, grad_branch, grad_gate_one, grad_shift_two, grad_scale_two = pull_second(
        (grad_out.reshape(shape_three), grad_hidden_two.reshape(shape_three))
    )
    branch_low = grad_branch.astype(jnp.bfloat16).reshape(token_count, D)
    grad_w_proj = jnp.einsum("nd,ne->de", attended, branch_low, preferred_element_type=jnp.float32)
    grad_b_proj = jnp.sum(branch_low.astype(jnp.float32), 0)
    grad_attended = jnp.einsum(
        "ne,de->nd", branch_low, w_proj, preferred_element_type=jnp.float32
    ).astype(jnp.bfloat16)
    grad_heads = grad_attended.reshape(row_count, local_len, HEADS, HEAD_DIM) * head_scale.astype(
        jnp.bfloat16
    )

    def attend_back(item):
        query_row, key_row, value_row, same_row, total_row, grad_row = item
        scores = raw_scores(query_row, key_row, same_row)
        probability = jnp.exp(scores - total_row[..., None])
        grad_prob = jnp.einsum(
            "qhe,khe->hqk", grad_row, heads_view(value_row), preferred_element_type=jnp.float32
        )
        inner = jnp.sum(probability * grad_prob, -1)
        grad_scores = (probability * (grad_prob - inner[..., None])).astype(jnp.bfloat16)
        grad_query = (
            jnp.einsum(
                "hqk,khe->qhe", grad_scores, heads_view(key_row), preferred_element_type=jnp.float32
            )
            * score_scale
        ).astype(jnp.bfloat16)
        return (grad_query.reshape(-1, D), inner)

    grad_query, inner_total = lax.map(
        attend_back, (query, key_rows, value_rows, same_crop, log_total, grad_heads)
    )
    query_all, grad_heads_all = (
        lax.all_gather(query, "seq", axis=1, tiled=True),
        lax.all_gather(grad_heads, "seq", axis=1, tiled=True),
    )
    total_all, inner_all = (
        lax.all_gather(log_total, "seq", axis=2, tiled=True),
        lax.all_gather(inner_total, "seq", axis=2, tiled=True),
    )
    same_owner = attend_keys[:, :, None] == attend_query[:, None, :]

    def owner_back(item):
        query_row, key_row, value_row, same_row, total_row, inner_row, grad_row = item
        scores = raw_scores(query_row, key_row, same_row)
        probability = jnp.exp(scores - total_row[..., None])
        grad_prob = jnp.einsum(
            "qhe,khe->hqk", grad_row, heads_view(value_row), preferred_element_type=jnp.float32
        )
        grad_scores = (probability * (grad_prob - inner_row[..., None])).astype(jnp.bfloat16)
        grad_key = (
            jnp.einsum(
                "hqk,qhe->khe",
                grad_scores,
                heads_view(query_row),
                preferred_element_type=jnp.float32,
            )
            * score_scale
        ).astype(jnp.bfloat16)
        grad_value = jnp.einsum(
            "hqk,qhe->khe",
            probability.astype(jnp.bfloat16),
            grad_row,
            preferred_element_type=jnp.float32,
        ).astype(jnp.bfloat16)
        return (grad_key.reshape(-1, D), grad_value.reshape(-1, D))

    key_grad, value_grad = lax.map(
        owner_back,
        (query_all, key_here, value_here, same_owner, total_all, inner_all, grad_heads_all),
    )
    grad_projected = jnp.concatenate([grad_query, key_grad, value_grad], -1).reshape(
        token_count, 3 * D
    )
    grad_w_qkv = jnp.einsum(
        "nd,ne->de", hidden_low, grad_projected, preferred_element_type=jnp.float32
    )
    grad_bias_qv = jnp.concatenate(
        [
            jnp.sum(grad_projected[:, :D].astype(jnp.float32), 0),
            jnp.sum(grad_projected[:, 2 * D :].astype(jnp.float32), 0),
        ]
    )
    grad_hidden_one = jnp.einsum(
        "ne,de->nd", grad_projected, w_qkv, preferred_element_type=jnp.float32
    ).reshape(shape_three)
    grad_token_two, grad_shift_one, grad_scale_one = pull_first(grad_hidden_one)
    grad_tokens = (grad_token_one + grad_token_two).astype(jnp.bfloat16)
    grad_per_token = jnp.concatenate(
        [
            grad_shift_one,
            grad_scale_one,
            grad_gate_one,
            grad_shift_two,
            grad_scale_two,
            grad_gate_two.reshape(shape_three),
        ],
        -1,
    )
    mod_parts = exact("rlc,rlm->rcm", crop_hot, grad_per_token)
    grad_mod = lax.psum_scatter(
        mod_parts.astype(jnp.bfloat16), "seq", scatter_dimension=2, tiled=True
    )
    grad_w_ada = jnp.einsum("rcd,rcm->dm", silu_low, grad_mod, preferred_element_type=jnp.float32)
    grad_b_ada = jnp.sum(grad_mod.astype(jnp.float32), (0, 1))
    grad_silu = jnp.einsum("rcm,dm->rcd", grad_mod, ada_full, preferred_element_type=jnp.float32)
    grad_condition = pull_silu(grad_silu)[0]
    grad_table = exact("rcn,rcd->nd", class_hot, grad_condition)
    bucket_count = lax.axis_size("bucket")
    grad_w_ada, grad_b_ada = (
        lax.psum_scatter(grad_w_ada, "bucket", scatter_dimension=0, tiled=True),
        lax.psum_scatter(
            grad_b_ada.reshape(bucket_count, -1), "bucket", scatter_dimension=0, tiled=True
        ),
    )
    part_table, part_qkv, part_bias_qv, part_proj, part_bproj = (
        lax.psum_scatter(grad_table, "bucket", scatter_dimension=1, tiled=True),
        lax.psum_scatter(grad_w_qkv, "bucket", scatter_dimension=1, tiled=True),
        lax.psum_scatter(grad_bias_qv, "bucket", scatter_dimension=0, tiled=True),
        lax.psum_scatter(grad_w_proj, "bucket", scatter_dimension=1, tiled=True),
        lax.psum_scatter(grad_b_proj, "bucket", scatter_dimension=0, tiled=True),
    )
    attention_sums = (
        lax.psum(part_table.astype(jnp.bfloat16), "seq").astype(jnp.float32),
        lax.psum(part_qkv.astype(jnp.bfloat16), "seq").astype(jnp.float32),
        lax.psum(part_bias_qv.astype(jnp.bfloat16), "seq").astype(jnp.float32),
        lax.psum(part_proj.astype(jnp.bfloat16), "seq").astype(jnp.float32),
        lax.psum(part_bproj.astype(jnp.bfloat16), "seq").astype(jnp.float32),
    )
    summed = tuple(attention_sums) + tuple(mlp_sums)
    return (
        output,
        grad_tokens,
        summed[0],
        grad_w_ada,
        grad_b_ada,
        summed[1],
        summed[2],
        summed[3],
        summed[4],
        summed[5],
        summed[6],
        summed[7],
        summed[8],
        summed[9],
    )


def solution(mesh):
    placed = (
        P("bucket", "seq", None),
        P("bucket", "seq", None),
        P("bucket", None),
        P("bucket"),
        P("bucket", None),
        P("bucket", None),
        P("bucket", None, None),
        P("bucket", None, None),
        P("bucket", "seq"),
        P(),
        P("bucket", "seq"),
        P("seq"),
        P(),
        P(),
        P(),
        P(),
        P(),
        P(),
        P(),
        P(),
        P(),
    )
    return jax.shard_map(
        body,
        mesh=mesh,
        in_specs=placed,
        out_specs=(
            P("bucket", "seq", None),
            P("bucket", "seq", None),
            P(None, "bucket"),
            P("bucket", "seq"),
            P("seq", "bucket"),
            P(None, "bucket"),
            P("bucket"),
            P(None, "bucket"),
            P("bucket"),
            P(None, "bucket"),
            P("bucket"),
            P("bucket", None),
            P("bucket"),
            P("bucket"),
        ),
        check_vma=False,
    )
```

profile of v0, /device:TPU:0, one launch (start us, length us, event | category | flops | bytes accessed | tf_op | source)
XLA Modules:
  0.0 1123.7 jit_solution(7249561307434286096)
XLA Ops:
  8.0 48.0 %all_gather.24 = bf16[384,1152]{1,0:T(8,128)(2,1)S(1)} all-gather(bf16[24,1152]{1,0:T(8,128)(2,1)} %param.37), channel_id=1, replica_groups=mesh['bucket'=16,'seq'=2] {'bucket'}, dimensions={0}, use_global_device_ids=true | all-gather | bytes 940032 | tf_op jit(solution)/shard_map/all_gather | solution.py:81
  62.3 6.3 fusion.91
  90.9 4.5 fusion.89
  95.4 19.8 %while.36 = (s32[]{:T(128)}, f32[4,256,6,64]{1,3,2,0:T(8,128)}, f32[4,6,256]{2,1,0:T(8,128)S(1)}, bf16[4,512,384]{1,2,0:T(8,128)(2,1)}, pred[4,256,512]{2,1,0:T(...) while((s32[]{:T(128)}, f32[4,256,6,64]{1,3,2,0:T(8,128)}, ...), condition=%wide.region_5.6_spmd, body=%wide.region_2.5_spmd.sunk | while | flops 210762240 | bytes 13490789 | solution.py:134
  121.8 3.1 fusion.103
  125.3 3.5 fusion.47
  128.9 3.6 fusion.69
  132.6 7.4 convert_reduce_fusion
  146.7 2.7 convert_reduce_fusion.3
  155.1 23.7 %while.37 = (s32[]{:T(128)}, bf16[4,256,384]{2,1,0:T(8,128)(2,1)S(1)}, f32[4,6,256]{2,1,0:T(8,128)S(1)}, bf16[4,512,384]{1,2,0:T(8,128)(2,1)}, pred[4,256,512]{2...) while((s32[]{:T(128)}, ...), condition=%wide.region_13.14_spmd, body=%wide.region_11.13_spmd.sunk | while | flops 310835712 | bytes 20830336 | solution.py:229
  184.3 2.9 copy.76
  189.2 64.5 %while.38 = (s32[]{:T(128)}, bf16[4,256,384]{2,1,0:T(8,128)(2,1)}, bf16[4,256,384]{2,1,0:T(8,128)(2,1)}, bf16[4,512,384]{1,2,0:T(8,128)(2,1)}, pred[4,512,256]{2...) while((s32[]{:T(128)}, bf16[4,256,384]{2,1,0:T(8,128)(2,1)}, ...), condition=%wide.region_15.16_spmd, body=%wide.region_14.15_spmd.sunk | while | flops 410812416 | bytes 16132277 | solution.py:267
  200.5 3.2 fusion.198
  216.6 3.2 fusion.198
  232.6 3.2 fusion.198
  248.6 3.2 fusion.198
  257.0 4.6 convert_reduce_fusion.2
  264.1 3.1 fusion.56
  272.1 3.1 convolution_convert_fusion
  279.7 2.6 fusion.110
  282.6 5.1 fusion.112
  288.9 5.1 fusion.111
  300.0 4.3 convolution_bitcast_fusion
  308.0 108.7 %reduce-scatter.28.cloned.1.call-done = f32[384,24]{0,1:T(8,128)} async-done(((f32[384,384]{0,1:T(8,128)}), f32[384,24]{0,1:T(8,128)}) %reduce-scatter.28.cloned.1.call-update) | async-done | bytes 36880
  419.8 129.3 %reduce-scatter.20.cloned.1.call-done = f32[96,384]{1,0:T(8,128)} async-done(((f32[1536,384]{1,0:T(8,128)}), f32[96,384]{1,0:T(8,128)}) %reduce-scatter.20.cloned.1.call-update) | async-done | bytes 147472 | tf_op jit(solution)/shard_map/reduce_scatter | solution.py:188
  550.6 131.7 %reduce-scatter.18.cloned.1.call-done = f32[384,96]{0,1:T(8,128)} async-done(((f32[384,1536]{0,1:T(8,128)}), f32[384,96]{0,1:T(8,128)}) %reduce-scatter.18.cloned.1.call-update) | async-done | bytes 147472 | tf_op jit(solution)/shard_map/reduce_scatter | solution.py:186
  684.1 75.1 %all-reduce.9 = (f32[16,72]{1,0:T(8,128)S(1)}, bf16[768]{0:T(1024)(128)(2,1)S(1)}, bf16[384]{0:T(512)(128)(2,1)S(1)}, bf16[1536]{0:T(1024)(128)(2,1)S(1)}, bf16[...) all-reduce(f32[16,72]{1,0:T(8,128)S(1)} %reshape.261, ...), channel_id=5, replica_groups=mesh['bucket'=16,'seq'=2] {'bucket'}, use_global_device_ids=true, to_apply=%region_23.24.clone | all-reduce | flops 4608 | bytes 29952
  762.2 48.7 %reduce-scatter.16.cloned.1.call-done = f32[1000,24]{0,1:T(8,128)} async-done(((f32[1000,384]{0,1:T(8,128)}), f32[1000,24]{0,1:T(8,128)}) %reduce-scatter.16.cloned.1.call-update) | async-done | bytes 96016 | tf_op jit(solution)/shard_map/reduce_scatter | solution.py:316
  812.4 128.9 %reduce-scatter.26.cloned.1.call-done = f32[384,72]{0,1:T(8,128)} async-done(((f32[384,1152]{0,1:T(8,128)}), f32[384,72]{0,1:T(8,128)}) %reduce-scatter.26.cloned.1.call-update) | async-done | bytes 110608
  945.7 15.5 %all-reduce.17.cloned.1.call-done = (bf16[384,96]{0,1:T(8,128)(2,1)}, bf16[96,384]{1,0:T(8,128)(2,1)}) async-done(((bf16[384,96]{0,1:T(8,128)(2,1)}, bf16[96,384]{1,0:T(8,128)(2,1)}), (bf16[384,96]{0,1:T(8,128)(2,1)}, bf16[96,384]{1,0:T(8,128)(2,1)})) %all-reduce.17.cloned.1.call-update) | async-done | bytes 147472 | tf_op jit(solution)/shard_map/psum | solution.py:193
  964.3 20.3 %all-reduce.15.cloned.1.call-done = (bf16[1000,24]{0,1:T(8,128)(2,1)}, bf16[384,72]{0,1:T(8,128)(2,1)}, bf16[48]{0:T(256)(128)(2,1)}, bf16[384,24]{0,1:T(8,128)(...) async-done(((bf16[1000,24]{0,1:T(8,128)(2,1)}, bf16[384,72]{0,1:T(8,128)(2,1)}, bf16[48]{0:T(256)(128)(2,1)}, ...) | async-done | bytes 122176 | tf_op jit(solution)/shard_map/psum | solution.py:323
  994.6 122.4 %reduce-scatter.24.cloned.1.call-done = f32[24,1152]{1,0:T(8,128)} async-done(((f32[384,1152]{1,0:T(8,128)}), f32[24,1152]{1,0:T(8,128)}) %reduce-scatter.24.cloned.1.call-update) | async-done | bytes 110608
  (415 shorter events, 202.1 us)
Async XLA Ops:
  7.2 118.1 %copy-start = (bf16[384,1536]{1,0:T(8,128)(2,1)S(1)}, bf16[384,1536]{1,0:T(8,128)(2,1)}, u32[]{:S(2)}) copy-start(bf16[384,1536]{1,0:T(8,128)(2,1)} %param.43) | copy-start | bytes 3538948
  7.2 88.2 %all-gather.5.cloned.1.call-start = ((), (), s32[]{:S(2)}) async-start(), calls=%async_computation.7 | async-start | bytes 2359296 | tf_op jit(solution)/shard_map/all_gather | solution.py:105
  8.0 52.9 %copy-start.6 = (bf16[4,256,384]{2,1,0:T(8,128)(2,1)S(1)}, bf16[4,256,384]{2,1,0:T(8,128)(2,1)}, u32[]{:S(2)}) copy-start(bf16[4,256,384]{2,1,0:T(8,128)(2,1)} %param.27) | copy-start | bytes 2359300
  61.2 7.4 copy-start.37
  62.3 6.4 copy-start.43
  62.3 28.6 %copy-start.39 = (s32[4,256]{1,0:T(4,128)}, s32[4,256]{1,0:T(4,128)S(1)}, u32[]{:S(2)}) copy-start(s32[4,256]{1,0:T(4,128)S(1)} %constant_dynamic-slice_fusion.10) | copy-start | bytes 12292
  76.3 19.2 %all-gather.7.cloned.1.call-start = ((), (), s32[]{:S(2)}) async-start(), calls=%async_computation.8 | async-start | bytes 2359296 | tf_op jit(solution)/shard_map/all_gather | solution.py:104
  79.0 4.3 copy-start.54
  79.0 105.3 %all-gather.11.cloned.1.call-start = ((), (), s32[]{:S(2)}) async-start(), calls=%async_computation.10 | async-start | bytes 2359296 | tf_op jit(solution)/shard_map/all_gather | solution.py:234
  89.7 57.0 %copy-start.47 = (f32[4,256]{1,0:T(4,128)}, f32[4,256]{1,0:T(4,128)S(1)}, u32[]{:S(2)}) copy-start(f32[4,256]{1,0:T(4,128)S(1)} %dynamic-slice_convert_fusion) | copy-start | bytes 12292
  118.8 6.4 slice-start
  121.4 23.1 %copy-start.2 = (f32[4,256,384]{2,1,0:T(8,128)}, f32[4,256,384]{2,1,0:T(8,128)S(1)}, u32[]{:S(2)}) copy-start(f32[4,256,384]{2,1,0:T(8,128)S(1)} %get-tuple-element.312) | copy-start | bytes 4718596
  121.4 23.1 %copy-start.35 = (f32[4,256]{1,0:T(4,128)}, f32[4,256]{1,0:T(4,128)S(1)}, u32[]{:S(2)}) copy-start(f32[4,256]{1,0:T(4,128)S(1)} %broadcast_multiply_fusion.1) | copy-start | bytes 12292
  121.8 22.7 %copy-start.41 = (f32[4,256]{1,0:T(4,128)}, f32[4,256]{1,0:T(4,128)S(1)}, u32[]{:S(2)}) copy-start(f32[4,256]{1,0:T(4,128)S(1)} %fusion.99) | copy-start | bytes 12292
  132.5 7.4 copy-start.69
  132.6 7.4 copy-start.52
  132.6 7.4 copy-start.64
  153.1 34.1 %all-gather.9.cloned.1.call-start = ((), (), s32[]{:S(2)}) async-start(), calls=%async_computation.9 | async-start | bytes 2359296 | tf_op jit(solution)/shard_map/all_gather | solution.py:233
  153.7 140.4 %reduce-scatter.22.cloned.1.call-start = ((), (), s32[]{:S(2)}) async-start(), calls=%async_computation.14 | async-start | bytes 884736
  257.0 4.6 copy-start.50
  257.0 4.7 copy-start.44
  279.6 137.1 %reduce-scatter.28.cloned.1.call-start = ((), (), s32[]{:S(2)}) async-start(), calls=%async_computation.17 | async-start | bytes 626688
  282.4 266.7 %reduce-scatter.20.cloned.1.call-start = ((), (), s32[]{:S(2)}) async-start(), calls=%async_computation.13 | async-start | bytes 2506752 | tf_op jit(solution)/shard_map/reduce_scatter | solution.py:188
  287.8 394.6 %reduce-scatter.18.cloned.1.call-start = ((), (), s32[]{:S(2)}) async-start(), calls=%async_computation.12 | async-start | bytes 2506752 | tf_op jit(solution)/shard_map/reduce_scatter | solution.py:186
  294.0 516.8 %reduce-scatter.16.cloned.1.call-start = ((), (), s32[]{:S(2)}) async-start(), calls=%async_computation.11 | async-start | bytes 1671168 | tf_op jit(solution)/shard_map/reduce_scatter | solution.py:316
  300.0 641.3 %reduce-scatter.26.cloned.1.call-start = ((), (), s32[]{:S(2)}) async-start(), calls=%async_computation.16 | async-start | bytes 1880064
  304.4 656.8 %all-reduce.17.cloned.1.call-start = ((), (), s32[]{:S(2)}) async-start(), calls=%async_computation.19 | async-start | bytes 294912 | tf_op jit(solution)/shard_map/psum | solution.py:193
  306.9 377.2 %copy-start.57 = (f32[384]{0:T(512)S(1)}, f32[384]{0:T(512)}, u32[]{:S(2)}) copy-start(f32[384]{0:T(512)} %get-tuple-element.309) | copy-start | bytes 4612
  306.9 377.2 %copy-start.59 = (f32[1536]{0:T(1024)S(1)}, f32[1536]{0:T(1024)}, u32[]{:S(2)}) copy-start(f32[1536]{0:T(1024)} %get-tuple-element.345) | copy-start | bytes 18436
  683.9 300.8 %all-reduce.15.cloned.1.call-start = ((), (), s32[]{:S(2)}) async-start(), calls=%async_computation.18 | async-start | bytes 250880 | tf_op jit(solution)/shard_map/psum | solution.py:323
  942.8 174.2 %reduce-scatter.24.cloned.1.call-start = ((), (), s32[]{:S(2)}) async-start(), calls=%async_computation.15 | async-start | bytes 1880064
  942.8 174.2 %copy-start.1 = (bf16[384,1536]{1,0:T(8,128)(2,1)S(1)}, bf16[384,1536]{1,0:T(8,128)(2,1)}, u32[]{:S(2)}) copy-start(bf16[384,1536]{1,0:T(8,128)(2,1)} %param.43) | copy-start | bytes 3538948
  (61 other events, 155.7 us)
Sparse Core Ops, SparseCore 0:
  76.4 5.6 all-gather.4
  83.6 10.8 all-gather.6
  153.2 9.8 all-gather.10
  164.5 10.8 all-gather.8
  279.8 8.2 reduce-scatter.21
  293.3 123.4 reduce-scatter.27
  421.7 127.3 reduce-scatter.19
  554.7 127.5 reduce-scatter.17
  687.1 123.7 reduce-scatter.15
  815.6 125.6 reduce-scatter.25
  944.2 16.9 all-reduce.16
  965.0 19.5 all-reduce.14
  990.1 126.8 reduce-scatter.23
where the time goes:
time: 1130 us; the launch traced here: 1120 us
  waiting for transfers between devices  706 us (62%)
  blocking collectives  129 us (11%)
  matrix products  112 us (10%)
  local copies, waits for them, and re-layouts  92.8 us (8%)
  other arithmetic  64.4 us (6%)
  between operations  17.1 us (2%)
    unnamed x17, waiting for transfers between devices  361 us
    reduce_scatter x1, waiting for transfers between devices, body(): lax.psum_scatter(grad_w_fc1, 'bucket', scatter_dimension=1, tiled=True)  132 us
    reduce_scatter x1, waiting for transfers between devices, body(): lax.psum_scatter(grad_w_fc2, 'bucket', scatter_dimension=0, tiled=True)  129 us
    unnamed x1, blocking collectives  75.1 us
    reduce_scatter x1, waiting for transfers between devices, body(): lax.psum_scatter(grad_table, 'bucket', scatter_dimension=1, tiled=True)  48.7 us
    all_gather x1, blocking collectives, body(): ada_full = lax.all_gather(w_ada, 'bucket', axis=0, tiled=True)  48 us
    unnamed x161, local copies, waits for them, and re-layouts  27.3 us
    dynamic_slice x24, local copies, waits for them, and re-layouts, body(): lax.map(attend, (query, key_rows, value_rows, same_crop))  24.4 us
  transfers between devices with their start and end apart: 13, of which 8 were waited for; matrix products, arithmetic and copies ran while one was open for 9% of the time, Pallas kernels for 0%

commit v1 on v0

--- a/solution.py
+++ b/solution.py
@@ -78,7 +78,9 @@
     crop_here = lax.dynamic_slice_in_dim(segment_ids, first_pos, local_len, 1)
     crop_hot = (crop_here[:, :, None] == jnp.arange(CROPS, dtype=jnp.int32)).astype(jnp.float32)
     class_hot = (classes[:, :, None] == jnp.arange(NCLASS, dtype=jnp.int32)).astype(jnp.float32)
-    ada_full = lax.all_gather(w_ada, "bucket", axis=0, tiled=True)
+    ada_full = jnp.concatenate(
+        lax.all_to_all(jnp.stack([w_ada] * lax.axis_size("bucket")), "bucket", 0, 0), axis=0
+    )
     condition = time_embed(timesteps) + exact(
         "rcn,nd->rcd", class_hot, class_table.astype(jnp.float32)
     )

time: 1130 us -> 1110 us (0.982)
  blocking collectives: 129 us -> 81.1 us
  waiting for transfers between devices: 706 us -> 738 us
    all_gather x1 -> x0, blocking collectives: 48 us -> none  [body(): ada_full = lax.all_gather(w_ada, 'bucket', axis=0, tiled=True)]
    all_to_all x0 -> x1, waiting for transfers between devices: none -> 19.7 us  [body(): lax.all_to_all(jnp.stack([w_ada] * lax.axis_size('bucket')), 'bucket', 0, 0)]
    all_gather x1, waiting for transfers between devices: 0.01 us -> 11.8 us  [body(): lax.all_gather(key_here, 'seq', axis=1, tiled=True)]
    unnamed x161 -> x171, local copies, waits for them, and re-layouts: 27.3 us -> 25.6 us
  transfers between devices with their start and end apart: 13 -> 14, of which waited for: 8 -> 10; matrix products, arithmetic and copies ran while one was open for 9% -> 8% of each run, Pallas kernels for 0% -> 0%
where the time goes in v1:
time: 1110 us
  waiting for transfers between devices  738 us (66%)
  matrix products  111 us (10%)
  local copies, waits for them, and re-layouts  94.1 us (8%)
  blocking collectives  81.1 us (7%)
  other arithmetic  54.8 us (5%)
  between operations  17.4 us (2%)
    unnamed x17, waiting for transfers between devices  361 us
    reduce_scatter x1, waiting for transfers between devices, body(): lax.psum_scatter(grad_w_fc1, 'bucket', scatter_dimension=1, tiled=True)  132 us
    reduce_scatter x1, waiting for transfers between devices, body(): lax.psum_scatter(grad_w_fc2, 'bucket', scatter_dimension=0, tiled=True)  129 us
    unnamed x1, blocking collectives  75.2 us
    reduce_scatter x1, waiting for transfers between devices, body(): lax.psum_scatter(grad_table, 'bucket', scatter_dimension=1, tiled=True)  48.7 us
    unnamed x171, local copies, waits for them, and re-layouts  25.6 us
    dynamic_slice x24, local copies, waits for them, and re-layouts, body(): lax.map(attend, (query, key_rows, value_rows, same_crop))  24.4 us
  transfers between devices with their start and end apart: 14, of which 10 were waited for; matrix products, arithmetic and copies ran while one was open for 8% of the time, Pallas kernels for 0%

profile of v1, /device:TPU:0, one launch (start us, length us, event | category | flops | bytes accessed | tf_op | source)
XLA Modules:
  0.0 1107.1 jit_solution(8975024728227956439)
XLA Ops:
  9.2 8.4 all-to-all-start
  19.4 19.7 %all-to-all-done = bf16[16,24,1152]{2,1,0:T(8,128)(2,1)S(1)} async-done(((bf16[16,24,1152]{2,1,0:T(8,128)(2,1)}), bf16[16,24,1152]{2,1,0:T(8,128)(2,1)S(1)}, u32[]{:S(2)}, u32[]{:S(2)}) %all-to-all-start) | async-done | bytes 884768 | tf_op jit(solution)/shard_map/all_to_all | solution.py:82
  41.4 6.3 fusion.88
  60.5 4.6 fusion.86
  66.4 11.8 %all-gather.7.cloned.1.call-done = bf16[4,512,384]{1,2,0:T(8,128)(2,1)} async-done(((bf16[4,256,384]{1,2,0:T(8,128)(2,1)}), bf16[4,512,384]{1,2,0:T(8,128)(2,1)}) %all-gather.7.cloned.1.call-update) | async-done | bytes 1572880 | tf_op jit(solution)/shard_map/all_gather | solution.py:106
  78.2 19.8 %while.36 = (s32[]{:T(128)}, f32[4,256,6,64]{1,3,2,0:T(8,128)}, f32[4,6,256]{2,1,0:T(8,128)S(1)}, bf16[4,512,384]{1,2,0:T(8,128)(2,1)}, pred[4,256,512]{2,1,0:T(...) while((s32[]{:T(128)}, f32[4,256,6,64]{1,3,2,0:T(8,128)}, ...), condition=%wide.region_5.6_spmd, body=%wide.region_2.5_spmd.sunk | while | flops 210762240 | bytes 13490789 | solution.py:136
  104.6 3.1 fusion.100
  108.1 3.5 fusion.47
  111.7 3.6 fusion.69
  115.3 7.4 convert_reduce_fusion
  137.3 23.6 %while.37 = (s32[]{:T(128)}, bf16[4,256,384]{2,1,0:T(8,128)(2,1)S(1)}, f32[4,6,256]{2,1,0:T(8,128)S(1)}, bf16[4,512,384]{1,2,0:T(8,128)(2,1)}, pred[4,256,512]{2...) while((s32[]{:T(128)}, ...), condition=%wide.region_13.14_spmd, body=%wide.region_11.13_spmd.sunk | while | flops 310835712 | bytes 20830336 | solution.py:231
  166.5 2.9 copy.76
  171.3 64.5 %while.38 = (s32[]{:T(128)}, bf16[4,256,384]{2,1,0:T(8,128)(2,1)}, bf16[4,256,384]{2,1,0:T(8,128)(2,1)}, bf16[4,512,384]{1,2,0:T(8,128)(2,1)}, pred[4,512,256]{2...) while((s32[]{:T(128)}, bf16[4,256,384]{2,1,0:T(8,128)(2,1)}, ...), condition=%wide.region_15.16_spmd, body=%wide.region_14.15_spmd.sunk | while | flops 410812416 | bytes 16132277 | solution.py:269
  182.7 3.2 fusion.198
  198.8 3.2 fusion.198
  214.8 3.2 fusion.198
  230.8 3.2 fusion.198
  239.2 4.6 convert_reduce_fusion.2
  246.3 3.1 fusion.56
  254.3 3.1 convolution_convert_fusion
  264.8 5.1 fusion.110
  271.0 5.1 fusion.109
  282.2 4.4 convolution_bitcast_fusion
  290.2 109.6 %reduce-scatter.28.cloned.1.call-done = f32[384,24]{0,1:T(8,128)} async-done(((f32[384,384]{0,1:T(8,128)}), f32[384,24]{0,1:T(8,128)}) %reduce-scatter.28.cloned.1.call-update) | async-done | bytes 36880
  402.9 129.4 %reduce-scatter.20.cloned.1.call-done = f32[96,384]{1,0:T(8,128)} async-done(((f32[1536,384]{1,0:T(8,128)}), f32[96,384]{1,0:T(8,128)}) %reduce-scatter.20.cloned.1.call-update) | async-done | bytes 147472 | tf_op jit(solution)/shard_map/reduce_scatter | solution.py:190
  533.9 131.9 %reduce-scatter.18.cloned.1.call-done = f32[384,96]{0,1:T(8,128)} async-done(((f32[384,1536]{0,1:T(8,128)}), f32[384,96]{0,1:T(8,128)}) %reduce-scatter.18.cloned.1.call-update) | async-done | bytes 147472 | tf_op jit(solution)/shard_map/reduce_scatter | solution.py:188
  667.5 75.2 %all-reduce.9 = (f32[16,72]{1,0:T(8,128)S(1)}, bf16[768]{0:T(1024)(128)(2,1)S(1)}, bf16[384]{0:T(512)(128)(2,1)S(1)}, bf16[1536]{0:T(1024)(128)(2,1)S(1)}, bf16[...) all-reduce(f32[16,72]{1,0:T(8,128)S(1)} %reshape.267, ...), channel_id=5, replica_groups=mesh['bucket'=16,'seq'=2] {'bucket'}, use_global_device_ids=true, to_apply=%region_23.24.clone | all-reduce | flops 4608 | bytes 29952
  745.7 48.7 %reduce-scatter.16.cloned.1.call-done = f32[1000,24]{0,1:T(8,128)} async-done(((f32[1000,384]{0,1:T(8,128)}), f32[1000,24]{0,1:T(8,128)}) %reduce-scatter.16.cloned.1.call-update) | async-done | bytes 96016 | tf_op jit(solution)/shard_map/reduce_scatter | solution.py:318
  795.9 128.8 %reduce-scatter.26.cloned.1.call-done = f32[384,72]{0,1:T(8,128)} async-done(((f32[384,1152]{0,1:T(8,128)}), f32[384,72]{0,1:T(8,128)}) %reduce-scatter.26.cloned.1.call-update) | async-done | bytes 110608
  929.2 15.4 %all-reduce.17.cloned.1.call-done = (bf16[384,96]{0,1:T(8,128)(2,1)}, bf16[96,384]{1,0:T(8,128)(2,1)}) async-done(((bf16[384,96]{0,1:T(8,128)(2,1)}, bf16[96,384]{1,0:T(8,128)(2,1)}), (bf16[384,96]{0,1:T(8,128)(2,1)}, bf16[96,384]{1,0:T(8,128)(2,1)})) %all-reduce.17.cloned.1.call-update) | async-done | bytes 147472 | tf_op jit(solution)/shard_map/psum | solution.py:195
  947.7 20.3 %all-reduce.15.cloned.1.call-done = (bf16[1000,24]{0,1:T(8,128)(2,1)}, bf16[384,72]{0,1:T(8,128)(2,1)}, bf16[48]{0:T(256)(128)(2,1)}, bf16[384,24]{0,1:T(8,128)(...) async-done(((bf16[1000,24]{0,1:T(8,128)(2,1)}, bf16[384,72]{0,1:T(8,128)(2,1)}, bf16[48]{0:T(256)(128)(2,1)}, ...) | async-done | bytes 122176 | tf_op jit(solution)/shard_map/psum | solution.py:325
  978.0 122.4 %reduce-scatter.24.cloned.1.call-done = f32[24,1152]{1,0:T(8,128)} async-done(((f32[384,1152]{1,0:T(8,128)}), f32[24,1152]{1,0:T(8,128)}) %reduce-scatter.24.cloned.1.call-update) | async-done | bytes 110608
  (427 shorter events, 197.5 us)
Async XLA Ops:
  7.2 100.9 %copy-start = (bf16[384,1536]{1,0:T(8,128)(2,1)S(1)}, bf16[384,1536]{1,0:T(8,128)(2,1)}, u32[]{:S(2)}) copy-start(bf16[384,1536]{1,0:T(8,128)(2,1)} %param.43) | copy-start | bytes 3538948
  7.2 10.5 copy-start.67
  7.2 10.5 copy-start.62
  7.2 10.6 copy-start.52
  7.2 10.6 copy-start.6
  9.2 9.3 copy-start.61
  9.2 9.9 copy-start.57
  9.2 29.9 %all-to-all-start = ((bf16[16,24,1152]{2,1,0:T(8,128)(2,1)}), bf16[16,24,1152]{2,1,0:T(8,128)(2,1)S(1)}, u32[]{:S(2)}, u32[]{:S(2)}) async-start(bf16[16,24,1152]{2,1,0:T(8,128)(2,1)} %stack.2), calls=%async_computation | async-start | bytes 1769472 | tf_op jit(solution)/shard_map/all_to_all | solution.py:82
  17.7 48.8 %all-gather.5.cloned.1.call-start = ((), (), s32[]{:S(2)}) async-start(), calls=%async_computation.8 | async-start | bytes 2359296 | tf_op jit(solution)/shard_map/all_gather | solution.py:107
  17.8 42.6 %copy-start.40 = (s32[4,256]{1,0:T(4,128)}, s32[4,256]{1,0:T(4,128)S(1)}, u32[]{:S(2)}) copy-start(s32[4,256]{1,0:T(4,128)S(1)} %constant_dynamic-slice_fusion.10) | copy-start | bytes 12292
  18.1 29.6 %copy-start.38 = (f32[4,256]{1,0:T(4,128)}, f32[4,256]{1,0:T(4,128)S(1)}, u32[]{:S(2)}) copy-start(f32[4,256]{1,0:T(4,128)S(1)} %broadcast_multiply_fusion.2) | copy-start | bytes 12292
  18.6 29.1 %copy-start.44 = (f32[4,256]{1,0:T(4,128)}, f32[4,256]{1,0:T(4,128)S(1)}, u32[]{:S(2)}) copy-start(f32[4,256]{1,0:T(4,128)S(1)} %fusion.95) | copy-start | bytes 12292
  19.4 28.3 %copy-start.33 = (f32[4,8,384]{2,1,0:T(8,128)}, f32[4,8,384]{2,1,0:T(8,128)S(1)}, u32[]{:S(2)}) copy-start(f32[4,8,384]{2,1,0:T(8,128)S(1)} %convolution_add_fusion.3) | copy-start | bytes 147460
  56.2 22.0 %all-gather.7.cloned.1.call-start = ((), (), s32[]{:S(2)}) async-start(), calls=%async_computation.9 | async-start | bytes 2359296 | tf_op jit(solution)/shard_map/all_gather | solution.py:106
  59.1 107.5 %all-gather.11.cloned.1.call-start = ((), (), s32[]{:S(2)}) async-start(), calls=%async_computation.11 | async-start | bytes 2359296 | tf_op jit(solution)/shard_map/all_gather | solution.py:236
  60.0 69.4 %copy-start.48 = (f32[4,256]{1,0:T(4,128)}, f32[4,256]{1,0:T(4,128)S(1)}, u32[]{:S(2)}) copy-start(f32[4,256]{1,0:T(4,128)S(1)} %dynamic-slice_convert_fusion) | copy-start | bytes 12292
  104.2 23.0 %copy-start.2 = (f32[4,256,384]{2,1,0:T(8,128)}, f32[4,256,384]{2,1,0:T(8,128)S(1)}, u32[]{:S(2)}) copy-start(f32[4,256,384]{2,1,0:T(8,128)S(1)} %get-tuple-element.312) | copy-start | bytes 4718596
  104.2 23.0 %copy-start.36 = (f32[4,256]{1,0:T(4,128)}, f32[4,256]{1,0:T(4,128)S(1)}, u32[]{:S(2)}) copy-start(f32[4,256]{1,0:T(4,128)S(1)} %broadcast_multiply_fusion.1) | copy-start | bytes 12292
  104.6 22.6 %copy-start.42 = (f32[4,256]{1,0:T(4,128)}, f32[4,256]{1,0:T(4,128)S(1)}, u32[]{:S(2)}) copy-start(f32[4,256]{1,0:T(4,128)S(1)} %fusion.96) | copy-start | bytes 12292
  135.8 33.6 %all-gather.9.cloned.1.call-start = ((), (), s32[]{:S(2)}) async-start(), calls=%async_computation.10 | async-start | bytes 2359296 | tf_op jit(solution)/shard_map/all_gather | solution.py:235
  137.0 139.2 %reduce-scatter.22.cloned.1.call-start = ((), (), s32[]{:S(2)}) async-start(), calls=%async_computation.15 | async-start | bytes 884736
  261.8 138.1 %reduce-scatter.28.cloned.1.call-start = ((), (), s32[]{:S(2)}) async-start(), calls=%async_computation.18 | async-start | bytes 626688
  264.5 267.8 %reduce-scatter.20.cloned.1.call-start = ((), (), s32[]{:S(2)}) async-start(), calls=%async_computation.14 | async-start | bytes 2506752 | tf_op jit(solution)/shard_map/reduce_scatter | solution.py:190
  269.9 395.8 %reduce-scatter.18.cloned.1.call-start = ((), (), s32[]{:S(2)}) async-start(), calls=%async_computation.13 | async-start | bytes 2506752 | tf_op jit(solution)/shard_map/reduce_scatter | solution.py:188
  276.2 518.2 %reduce-scatter.16.cloned.1.call-start = ((), (), s32[]{:S(2)}) async-start(), calls=%async_computation.12 | async-start | bytes 1671168 | tf_op jit(solution)/shard_map/reduce_scatter | solution.py:318
  282.1 642.5 %reduce-scatter.26.cloned.1.call-start = ((), (), s32[]{:S(2)}) async-start(), calls=%async_computation.17 | async-start | bytes 1880064
  286.6 658.0 %all-reduce.17.cloned.1.call-start = ((), (), s32[]{:S(2)}) async-start(), calls=%async_computation.20 | async-start | bytes 294912 | tf_op jit(solution)/shard_map/psum | solution.py:195
  289.1 378.4 %copy-start.59 = (f32[384]{0:T(512)S(1)}, f32[384]{0:T(512)}, u32[]{:S(2)}) copy-start(f32[384]{0:T(512)} %get-tuple-element.309) | copy-start | bytes 4612
  289.1 378.4 %copy-start.60 = (f32[1536]{0:T(1024)S(1)}, f32[1536]{0:T(1024)}, u32[]{:S(2)}) copy-start(f32[1536]{0:T(1024)} %get-tuple-element.345) | copy-start | bytes 18436
  667.3 300.7 %all-reduce.15.cloned.1.call-start = ((), (), s32[]{:S(2)}) async-start(), calls=%async_computation.19 | async-start | bytes 250880 | tf_op jit(solution)/shard_map/psum | solution.py:325
  926.2 174.2 %reduce-scatter.24.cloned.1.call-start = ((), (), s32[]{:S(2)}) async-start(), calls=%async_computation.16 | async-start | bytes 1880064
  926.3 174.2 %copy-start.1 = (bf16[384,1536]{1,0:T(8,128)(2,1)S(1)}, bf16[384,1536]{1,0:T(8,128)(2,1)}, u32[]{:S(2)}) copy-start(bf16[384,1536]{1,0:T(8,128)(2,1)} %param.43) | copy-start | bytes 3538948
  (67 other events, 183.6 us)
Sparse Core Ops, SparseCore 0:
  56.3 9.4 all-gather.4
  67.3 10.8 all-gather.6
  135.9 10.8 all-gather.10
  148.8 10.8 all-gather.8
  261.9 9.2 reduce-scatter.21
  276.4 123.4 reduce-scatter.27
  404.8 127.5 reduce-scatter.19
  538.0 127.6 reduce-scatter.17
  670.6 123.7 reduce-scatter.15
  799.1 125.5 reduce-scatter.25
  927.6 16.9 all-reduce.16
  948.4 19.5 all-reduce.14
  973.5 126.8 reduce-scatter.23
